TPU v7x, 128 devices: a whole 4x4x4 slice. The times are simulated.
128 devices in a mesh: row: 8 (over z, x_hi), col: 16 (over x_lo, y, core).
Axes of the slice: x: 4 (x_hi: 2, x_lo: 2; x = x_hi * 2 + x_lo), y: 4, z: 4, core: 2. Of those that a mesh axis runs over, the one named last changes fastest.
Arguments:
- factor: float32 [16384, 16384], P(('row', 'col')), as said below
- damping: float32 [16384], P(('row', 'col')), may hold values from 0.1 to 1
- gradients: float32 [3072, 128], replicated, may hold values from -6 to 6
- inverses: float32 [5, 512, 512], replicated, as said below
Outputs:
- updated: float32 [8, 8, 256, 4, 16, 256], P(None, 'row', None, None, 'col')
- panel_tiles: float32 [8, 8, 256, 512], P(None, 'row', 'col')
- solution: float32 [3072, 128], replicated
Inputs may be any that keep to these rules, and one draw needn't show every extreme that they name: `factor`: symmetric. `inverses`: one matrix for each diagonal block after the first.
All inputs are finite; a program needn't handle non-finite values.
Results may differ from a plain program's by a relative error of at most 0.0001.
Values sent between devices are 32-bit elements; how exact they have to be, the bound alone decides.
No kernel may reach another device: no remote copies, remote signals or barrier semaphores. Data moves between devices by JAX's collectives and lax.ppermute only.
A program may use at most 128 MiB of HBM per device.

v0:
```python
import jax
import jax.numpy as jnp
from jax import lax
from jax.sharding import PartitionSpec as P


def spread_2(block, axis, source):
    block = jnp.where(lax.axis_index(axis) == source, block, jnp.zeros_like(block))
    return lax.psum(block, axis)


def right_solve(corner_factor, panel_rows):
    return jax.scipy.linalg.solve_triangular(corner_factor, panel_rows.T, lower=True).T


def exact_dot(left, right):
    return jnp.dot(left, right, precision=lax.Precision.HIGHEST, preferred_element_type=jnp.float32)


def locate(block_index, position, axis_count, tile_size, block_width):
    piece_width = min(tile_size, block_width)
    pieces = block_width // piece_width
    first_tile = block_index * block_width // tile_size
    offset = block_index * block_width % tile_size
    turn_index = (position - first_tile) % axis_count
    is_valid = turn_index < pieces
    local_start = (first_tile + turn_index) // axis_count * tile_size + offset
    return (local_start, turn_index * piece_width, is_valid)


def place(segment, place_at, block_width, axis_dim):
    extent = list(segment.shape)
    extent[axis_dim] = block_width + segment.shape[axis_dim]
    buffer = jnp.zeros(tuple(extent), segment.dtype)
    filled = lax.dynamic_update_slice_in_dim(buffer, segment, place_at, axis_dim)
    return lax.slice_in_dim(filled, 0, block_width, axis=axis_dim)


def body(factor, damping, gradients, inverses):
    row_count = lax.axis_size("row")
    col_count = lax.axis_size("col")
    part_rows, order_size = factor.shape
    panel_width = inverses.shape[1]
    tile_size = order_size // (row_count * row_count)
    col_tiles = order_size // (col_count * tile_size)
    local_cols = col_tiles * tile_size
    local_rows = row_count * tile_size
    piece_width = min(tile_size, panel_width)
    share_rows = tile_size // col_count
    lead_share = panel_width // col_count
    row_index = lax.axis_index("row")
    col_index = lax.axis_index("col")
    first_col = (row_index * col_count + col_index) * part_rows
    square = lax.dynamic_slice_in_dim(factor, first_col, part_rows, 1) + jnp.diag(damping)
    damped = lax.dynamic_update_slice_in_dim(factor, square, first_col, 1)
    arranged = damped.reshape(part_rows, col_tiles, col_count, tile_size).transpose(2, 0, 1, 3)
    arranged = arranged.reshape(col_count, part_rows, local_cols)
    carried = None
    spread = lax.all_to_all(arranged, "col", split_axis=0, concat_axis=1, tiled=True)
    landed = lax.all_to_all(spread, "row", split_axis=1, concat_axis=0, tiled=True)
    local_block = landed.reshape(local_rows, local_cols)
    row_start, row_place, row_valid = locate(0, row_index, row_count, tile_size, panel_width)
    col_start, col_place, col_valid = locate(0, col_index, col_count, tile_size, panel_width)
    col_piece = lax.dynamic_slice_in_dim(local_block, col_start, piece_width, 1) * col_valid.astype(
        jnp.float32
    )
    contrib = place(col_piece, col_place, panel_width, 1)
    corner_piece = lax.dynamic_slice_in_dim(contrib, row_start, piece_width, 0) * row_valid.astype(
        jnp.float32
    )
    corner = lax.psum(place(corner_piece, row_place, panel_width, 0), ("row", "col"))
    corner_factor = jnp.linalg.cholesky(corner)
    panel_rows = lax.psum(contrib, "col")
    factor_rows = right_solve(corner_factor, panel_rows)
    own_factor = lax.dynamic_slice_in_dim(
        factor_rows.reshape(row_count, tile_size, panel_width),
        col_index * share_rows,
        share_rows,
        1,
    )
    grouped = factor_rows.reshape(col_tiles, col_count // row_count, tile_size, panel_width)
    picked = lax.dynamic_index_in_dim(grouped, col_index // row_count, 1, keepdims=False)
    picked = picked.reshape(local_cols, panel_width)
    factor_cols = spread_2(picked, "row", col_index % row_count)
    outer_part = lax.dot_general(
        factor_rows,
        factor_cols,
        (((1,), (1,)), ((), ())),
        precision=lax.Precision.HIGHEST,
        preferred_element_type=jnp.float32,
    )
    trailing = local_block - outer_part
    block_count = gradients.shape[0] // panel_width
    first_block = jax.scipy.linalg.solve_triangular(
        corner_factor, gradients[:panel_width], lower=True
    )
    solved = [first_block]
    known_cols = jnp.zeros((local_cols, gradients.shape[1]), jnp.float32)
    lead_start = col_index * lead_share
    first_share = lax.dynamic_slice_in_dim(first_block, lead_start, lead_share, 0)
    for block_index in range(1, block_count):
        if block_index > 1:
            put_start, put_place, put_valid = locate(
                block_index - 1, col_index, col_count, tile_size, panel_width
            )
            segment = lax.dynamic_slice_in_dim(solved[-1], put_place, piece_width, 0)
            current = lax.dynamic_slice_in_dim(known_cols, put_start, piece_width, 0)
            known_cols = lax.dynamic_update_slice_in_dim(
                known_cols, jnp.where(put_valid, segment, current), put_start, 0
            )
        block_start, block_place, block_valid = locate(
            block_index, row_index, row_count, tile_size, panel_width
        )
        lead_rows = lax.dynamic_slice_in_dim(factor_rows, block_start, piece_width, 0)
        lead_part = lax.dynamic_slice_in_dim(lead_rows, lead_start, lead_share, 1)
        partial_value = exact_dot(lead_part, first_share)
        if block_index > 1:
            schur_rows = lax.dynamic_slice_in_dim(trailing, block_start, piece_width, 0)
            partial_value = partial_value + exact_dot(schur_rows, known_cols)
        partial_value = partial_value * block_valid.astype(jnp.float32)
        summed = lax.psum(place(partial_value, block_place, panel_width, 0), ("row", "col"))
        right_side = gradients[block_index * panel_width : (block_index + 1) * panel_width]
        solved.append(exact_dot(inverses[block_index - 1], right_side - summed))
    solution = jnp.concatenate(solved, axis=0)
    updated = trailing.reshape(row_count, 1, tile_size, col_tiles, 1, tile_size)
    panel_tiles = own_factor.reshape(row_count, 1, share_rows, panel_width)
    return (updated, panel_tiles, solution)


def solution(mesh):
    return jax.shard_map(
        body,
        mesh=mesh,
        in_specs=(P(("row", "col"), None), P(("row", "col")), P(), P()),
        out_specs=(P(None, "row", None, None, "col", None), P(None, "row", "col", None), P()),
        check_vma=False,
    )
```

profile of v0, /device:TPU:1, one launch (start us, length us, event | category | flops | bytes accessed | tf_op | source)
XLA Modules:
  0.0 1456.4 jit_solution(4369769002759106836)
XLA Ops:
  7.2 7.6 copy.88
  16.3 9.2 copy.41
  25.5 10.0 copy.27
  35.5 100.9 %all_to_all.21 = f32[16,128,1024]{1,2,0:T(8,128)} all-to-all(f32[16,128,1024]{1,2,0:T(8,128)} %bitcast.143), channel_id=1, replica_groups=mesh['row'=8,'col'=16] {'col'}, dimensions={0} | all-to-all | bytes 16777216 | tf_op jit(solution)/shard_map/all_to_all | solution.py:59
  136.5 9.2 copy.28
  145.7 10.8 copy.29
  156.5 7.2 all-to-all-start.1
  163.9 94.4 %all-to-all-done.1 = f32[1,2048,1024]{2,0,1:T(1,128)} async-done(((f32[1,2048,1024]{2,0,1:T(1,128)}), f32[1,2048,1024]{2,0,1:T(1,128)}, u32[]{:S(2)}, u32[]{:S(2)}) %all-to-all-start.1) | async-done | bytes 8388640 | tf_op jit(solution)/shard_map/all_to_all | solution.py:60
  258.3 4.4 constant_dynamic-slice_fusion.2
  262.7 4.6 copy.40
  268.3 2.6 fusion.112
  273.2 145.4 %all-reduce.10.cloned.1.call-done = f32[512,512]{0,1:T(8,128)} async-done(((f32[512,512]{0,1:T(8,128)}), f32[512,512]{0,1:T(8,128)}) %all-reduce.10.cloned.1.call-update) | async-done | bytes 1048592 | tf_op jit(solution)/shard_map/psum | solution.py:71
  421.6 11.7 cholesky.85
  433.5 9.8 custom-call.34
  444.0 11.7 cholesky.180
  455.7 10.2 custom-call.35
  466.6 11.7 cholesky.201
  478.3 9.8 custom-call.36
  488.7 11.7 cholesky.218
  505.3 10.4 while.1
  506.0 2.0 bitcast_dynamic-update-slice_fusion.8
  515.7 40.1 %custom-call.37 = f32[4,128,128]{1,2,0:T(8,128)S(1)} custom-call(f32[4,128,128]{2,1,0:T(8,128)} %get-tuple-element.10), custom_call_target="InvertDiagBlocksLowerTriangular" | custom-call | tf_op jit(solution)/shard_map/jit(_solve_triangular)/triangular_solve | solution.py:13
  561.9 2.4 fusion.23
  564.3 2.2 convolution_subtract_fusion.1
  569.9 2.0 fusion.6
  573.1 4.4 pad_maximum_fusion
  577.4 6.6 reshape.97
  586.5 8.8 fusion.9
  600.7 6.1 copy.43
  608.1 119.9 %all-reduce.16.cloned.1.call-done = f32[512,128]{1,0:T(8,128)} async-done(((f32[512,128]{1,0:T(8,128)}), f32[512,128]{1,0:T(8,128)}) %all-reduce.16.cloned.1.call-update) | async-done | bytes 262160 | tf_op jit(solution)/shard_map/psum | solution.py:121
  728.0 3.4 bitcast_dynamic-update-slice_fusion.5
  731.4 102.9 %all-reduce.14.cloned.1.call-done = f32[1024,512]{0,1:T(8,128)} async-done(((f32[1024,512]{0,1:T(8,128)}), f32[1024,512]{0,1:T(8,128)}) %all-reduce.14.cloned.1.call-update) | async-done | bytes 2097168 | tf_op jit(solution)/shard_map/psum | solution.py:9
  834.3 20.1 %bitcast_subtract_fusion = f32[2048,1024]{1,0:T(8,128)S(1)} fusion(f32[1,2048,1024]{2,0,1:T(1,128)} %all-to-all-done.1, f32[1024,512]{0,1:T(8,128)} %all-reduce.14.cloned.1.call-done, f32[128,2048]{1,0:T(8,128)} %copy-done.2, f32[128,2048]{1,0:T(8,128)} %copy-done.1, f32[128,2048]{1,0:T(8,128)S(1)} %fusion.83, f32[128,2048]{1,0:T(8,128)S(1)} %fusion.23), kind=kOutput, calls=%fused_computation.2 | convolution fusion | flops 12890144768 | bytes 23068672 | tf_op jit(solution)/shard_map/dot_general | solution.py:85
  854.5 3.2 copy-done
  860.7 141.0 %all-reduce.18.cloned.1.call-done = f32[512,128]{1,0:T(8,128)} async-done(((f32[512,128]{1,0:T(8,128)}), f32[512,128]{1,0:T(8,128)}) %all-reduce.18.cloned.1.call-update) | async-done | bytes 262160 | tf_op jit(solution)/shard_map/psum | solution.py:121
  1001.7 3.4 bitcast_dynamic-update-slice_fusion.4
  1005.2 2.2 fusion.19
  1009.7 139.1 %all-reduce.20.cloned.1.call-done = f32[512,128]{1,0:T(8,128)} async-done(((f32[512,128]{1,0:T(8,128)}), f32[512,128]{1,0:T(8,128)}) %all-reduce.20.cloned.1.call-update) | async-done | bytes 262160 | tf_op jit(solution)/shard_map/psum | solution.py:121
  1148.8 3.4 bitcast_dynamic-update-slice_fusion.3
  1152.2 2.2 fusion.17
  1156.5 139.3 %all-reduce.22.cloned.1.call-done = f32[512,128]{1,0:T(8,128)} async-done(((f32[512,128]{1,0:T(8,128)}), f32[512,128]{1,0:T(8,128)}) %all-reduce.22.cloned.1.call-update) | async-done | bytes 262160 | tf_op jit(solution)/shard_map/psum | solution.py:121
  1295.8 3.4 bitcast_dynamic-update-slice_fusion.2
  1299.2 2.2 fusion.15
  1302.2 2.2 constant_dynamic-slice_fusion.1
  1305.8 13.5 reshape.120
  1319.3 123.6 %all-reduce.24.cloned.1.call-done = f32[512,128]{1,0:T(8,128)} async-done(((f32[512,128]{1,0:T(8,128)}), f32[512,128]{1,0:T(8,128)}) %all-reduce.24.cloned.1.call-update) | async-done | bytes 262160 | tf_op jit(solution)/shard_map/psum | solution.py:121
  1442.9 3.4 fusion.13
  1446.3 3.0 copy.38
  (117 shorter events, 49.4 us)
Async XLA Ops:
  7.2 7.6 copy-start.8
  156.5 101.7 %all-to-all-start.1 = ((f32[1,2048,1024]{2,0,1:T(1,128)}), f32[1,2048,1024]{2,0,1:T(1,128)}, u32[]{:S(2)}, u32[]{:S(2)}) async-start(f32[1,2048,1024]{2,0,1:T(1,128)} %copy.29), calls=%async_computation.1 | async-start | bytes 16777216 | tf_op jit(solution)/shard_map/all_to_all | solution.py:60
  163.7 254.8 %all-reduce.10.cloned.1.call-start = ((), (), s32[]{:S(2)}) async-start(), calls=%async_computation.2 | async-start | bytes 2097152 | tf_op jit(solution)/shard_map/psum | solution.py:71
  272.2 289.7 %all-reduce.12.cloned.1.call-start = ((), (), s32[]{:S(2)}) async-start(), calls=%async_computation.3 | async-start | bytes 8388608 | tf_op jit(solution)/shard_map/psum | solution.py:73
  272.9 455.0 %all-reduce.16.cloned.1.call-start = ((), (), s32[]{:S(2)}) async-start(), calls=%async_computation.5 | async-start | bytes 524288 | tf_op jit(solution)/shard_map/psum | solution.py:121
  559.7 1.5 copy-start.4
  561.2 0.6 copy-start.6
  561.9 5.7 copy-start.3
  569.9 7.5 copy-start.1
  573.0 4.4 copy-start.2
  586.1 248.2 %all-reduce.14.cloned.1.call-start = ((), (), s32[]{:S(2)}) async-start(), calls=%async_computation.4 | async-start | bytes 4194304 | tf_op jit(solution)/shard_map/psum | solution.py:9
  595.3 2.5 copy-start.5
  595.4 2.6 copy-start.7
  597.2 404.5 %all-reduce.18.cloned.1.call-start = ((), (), s32[]{:S(2)}) async-start(), calls=%async_computation.6 | async-start | bytes 524288 | tf_op jit(solution)/shard_map/psum | solution.py:121
  854.4 3.2 copy-start
  859.4 289.4 %all-reduce.20.cloned.1.call-start = ((), (), s32[]{:S(2)}) async-start(), calls=%async_computation.7 | async-start | bytes 524288 | tf_op jit(solution)/shard_map/psum | solution.py:121
  1008.1 287.7 %all-reduce.22.cloned.1.call-start = ((), (), s32[]{:S(2)}) async-start(), calls=%async_computation.8 | async-start | bytes 524288 | tf_op jit(solution)/shard_map/psum | solution.py:121
  1155.2 287.8 %all-reduce.24.cloned.1.call-start = ((), (), s32[]{:S(2)}) async-start(), calls=%async_computation.9 | async-start | bytes 524288 | tf_op jit(solution)/shard_map/psum | solution.py:121
Sparse Core Ops, SparseCore 0:
  272.3 146.2 all-reduce.9
  421.7 128.5 all-reduce.11
  586.2 141.7 all-reduce.15
  730.3 103.9 all-reduce.13
  859.5 142.1 all-reduce.17
  1008.2 140.4 all-reduce.19
  1155.3 140.4 all-reduce.21
  1302.3 140.5 all-reduce.23
where the time goes:
time: 1460 us
  waiting for transfers between devices  1010 us (69%)
  other arithmetic  136 us (9%)
  local copies, waits for them, and re-layouts  118 us (8%)
  blocking collectives  101 us (7%)
  matrix products  69.3 us (5%)
  between operations  18.1 us (1%)
    psum x5, waiting for transfers between devices, body(): lax.psum(place(partial_value, block_place, panel_width, 0), ('row', 'col'))  663 us
    psum x1, waiting for transfers between devices, body(): lax.psum(place(corner_piece, row_place, panel_width, 0), ('row', 'col'))  145 us
    psum x1, waiting for transfers between devices, spread_2(): return lax.psum(block, axis)  103 us
    all_to_all x1, blocking collectives, body(): lax.all_to_all(arranged, 'col', split_axis=0, concat_axis=1, tiled=True)  101 us
    all_to_all x1, waiting for transfers between devices, body(): lax.all_to_all(spread, 'row', split_axis=1, concat_axis=0, tiled=True)  94.4 us
    another operation x14, other arithmetic, body(): corner_factor = jnp.linalg.cholesky(corner)  78.7 us
    another operation x4, other arithmetic, right_solve(): jax.scipy.linalg.solve_triangular(corner_factor, panel_rows.T, lower=True)  44.6 us
    unnamed x28, local copies, waits for them, and re-layouts  38.7 us
  transfers between devices with their start and end apart: 9, of which 8 were waited for; matrix products, arithmetic and copies ran while one was open for 13% of the time, Pallas kernels for 0%

commit v1 on v0

--- a/solution.py
+++ b/solution.py
@@ -6,7 +6,7 @@
 
 def spread_2(block, axis, source):
     block = jnp.where(lax.axis_index(axis) == source, block, jnp.zeros_like(block))
-    return lax.psum(block, axis)
+    return jnp.sum(lax.all_gather(block, axis), axis=0)
 
 
 def right_solve(corner_factor, panel_rows):

time: 1460 us -> 1560 us (1.068)
  waiting for transfers between devices: 1010 us -> 1080 us
    all_gather x0 -> x1, waiting for transfers between devices: none -> 178 us  [spread_2(): return jnp.sum(lax.all_gather(block, axis), axis=0)]
    psum x1 -> x0, waiting for transfers between devices: 103 us -> none  [spread_2(): return lax.psum(block, axis)]
    unnamed x28 -> x27, local copies, waits for them, and re-layouts: 38.7 us -> 36.9 us
  transfers between devices with their start and end apart: 9 -> 9, of which waited for: 8 -> 8; matrix products, arithmetic and copies ran while one was open for 13% -> 12% of each run, Pallas kernels for 0% -> 0%
where the time goes in v1:
time: 1560 us; the launch traced here: 1550 us
  waiting for transfers between devices  1080 us (69%)
  other arithmetic  142 us (9%)
  local copies, waits for them, and re-layouts  123 us (8%)
  blocking collectives  101 us (6%)
  matrix products  81.6 us (5%)
  between operations  18.2 us (1%)
    psum x5, waiting for transfers between devices, body(): lax.psum(place(partial_value, block_place, panel_width, 0), ('row', 'col'))  661 us
    all_gather x1, waiting for transfers between devices, spread_2(): return jnp.sum(lax.all_gather(block, axis), axis=0)  178 us
    psum x1, waiting for transfers between devices, body(): lax.psum(place(corner_piece, row_place, panel_width, 0), ('row', 'col'))  145 us
    all_to_all x1, blocking collectives, body(): lax.all_to_all(arranged, 'col', split_axis=0, concat_axis=1, tiled=True)  101 us
    all_to_all x1, waiting for transfers between devices, body(): lax.all_to_all(spread, 'row', split_axis=1, concat_axis=0, tiled=True)  94.4 us
    another operation x14, other arithmetic, body(): corner_factor = jnp.linalg.cholesky(corner)  78.8 us
    another operation x4, other arithmetic, right_solve(): jax.scipy.linalg.solve_triangular(corner_factor, panel_rows.T, lower=True)  44.6 us
    unnamed x27, local copies, waits for them, and re-layouts  36.9 us
  transfers between devices with their start and end apart: 9, of which 8 were waited for; matrix products, arithmetic and copies ran while one was open for 12% of the time, Pallas kernels for 0%

profile of v1, /device:TPU:1, one launch (start us, length us, event | category | flops | bytes accessed | tf_op | source)
XLA Modules:
  0.0 1553.3 jit_solution(16054793109916458360)
XLA Ops:
  7.2 7.6 copy.92
  16.3 9.2 copy.46
  25.5 10.0 copy.29
  35.5 100.9 %all_to_all.21 = f32[16,128,1024]{1,2,0:T(8,128)} all-to-all(f32[16,128,1024]{1,2,0:T(8,128)} %bitcast.140), channel_id=1, replica_groups=mesh['row'=8,'col'=16] {'col'}, dimensions={0} | all-to-all | bytes 16777216 | tf_op jit(solution)/shard_map/all_to_all | solution.py:59
  136.5 9.2 copy.30
  145.7 10.9 copy.31
  156.6 7.2 all-to-all-start.1
  163.9 94.4 %all-to-all-done.1 = f32[1,2048,1024]{2,0,1:T(1,128)} async-done(((f32[1,2048,1024]{2,0,1:T(1,128)}), f32[1,2048,1024]{2,0,1:T(1,128)}, u32[]{:S(2)}, u32[]{:S(2)}) %all-to-all-start.1) | async-done | bytes 8388640 | tf_op jit(solution)/shard_map/all_to_all | solution.py:60
  258.3 4.4 constant_dynamic-slice_fusion.2
  262.7 4.6 copy.45
  268.3 2.6 fusion.111
  273.2 145.4 %all-reduce.9.cloned.1.call-done = f32[512,512]{0,1:T(8,128)} async-done(((f32[512,512]{0,1:T(8,128)}), f32[512,512]{0,1:T(8,128)}) %all-reduce.9.cloned.1.call-update) | async-done | bytes 1048592 | tf_op jit(solution)/shard_map/psum | solution.py:71
  421.6 11.7 cholesky.85
  433.5 9.8 custom-call.34
  444.0 11.7 cholesky.180
  455.7 10.2 custom-call.35
  466.6 11.7 cholesky.201
  478.4 9.8 custom-call.36
  488.8 11.7 cholesky.218
  505.5 10.9 while.1
  516.4 40.1 %custom-call.37 = f32[4,128,128]{1,2,0:T(8,128)S(1)} custom-call(f32[4,128,128]{2,1,0:T(8,128)} %get-tuple-element.10), custom_call_target="InvertDiagBlocksLowerTriangular" | custom-call | tf_op jit(solution)/shard_map/jit(_solve_triangular)/triangular_solve | solution.py:13
  562.6 2.4 fusion.22
  565.0 2.2 convolution_subtract_fusion.1
  573.8 4.4 pad_maximum_fusion
  578.2 6.6 reshape.107
  587.3 5.7 broadcast_select_fusion
  593.0 6.1 copy.34
  602.5 6.1 copy.47
  609.9 118.7 %all-reduce.13.cloned.1.call-done = f32[512,128]{1,0:T(8,128)} async-done(((f32[512,128]{1,0:T(8,128)}), f32[512,128]{1,0:T(8,128)}) %all-reduce.13.cloned.1.call-update) | async-done | bytes 262160 | tf_op jit(solution)/shard_map/psum | solution.py:121
  728.6 3.4 bitcast_dynamic-update-slice_fusion.5
  732.1 177.9 %all-gather.2.cloned.1.call-done = f32[8,1024,512]{2,1,0:T(8,128)} async-done(((f32[1,1024,512]{2,1,0:T(8,128)}), f32[8,1024,512]{2,1,0:T(8,128)}) %all-gather.2.cloned.1.call-update) | async-done | bytes 16777232 | tf_op jit(solution)/shard_map/all_gather | solution.py:9
  909.9 9.4 reduce_sum.9
  919.3 32.4 %bitcast_subtract_fusion = f32[2048,1024]{1,0:T(8,128)S(1)} fusion(f32[1,2048,1024]{2,0,1:T(1,128)} %all-to-all-done.1, f32[1024,512]{1,0:T(8,128)} %reduce_sum.9, f32[128,2048]{1,0:T(8,128)} %copy-done.2, f32[128,2048]{1,0:T(8,128)} %copy-done.1, f32[128,2048]{1,0:T(8,128)S(1)} %fusion.82, f32[128,2048]{1,0:T(8,128)S(1)} %fusion.22), kind=kOutput, calls=%fused_computation.2 | convolution fusion | flops 12890144768 | bytes 23068672 | tf_op jit(solution)/shard_map/dot_general | solution.py:85
  951.8 3.2 copy-done
  958.0 140.4 %all-reduce.15.cloned.1.call-done = f32[512,128]{1,0:T(8,128)} async-done(((f32[512,128]{1,0:T(8,128)}), f32[512,128]{1,0:T(8,128)}) %all-reduce.15.cloned.1.call-update) | async-done | bytes 262160 | tf_op jit(solution)/shard_map/psum | solution.py:121
  1098.4 3.4 bitcast_dynamic-update-slice_fusion.4
  1101.9 2.2 fusion.18
  1106.2 139.3 %all-reduce.17.cloned.1.call-done = f32[512,128]{1,0:T(8,128)} async-done(((f32[512,128]{1,0:T(8,128)}), f32[512,128]{1,0:T(8,128)}) %all-reduce.17.cloned.1.call-update) | async-done | bytes 262160 | tf_op jit(solution)/shard_map/psum | solution.py:121
  1245.5 3.4 bitcast_dynamic-update-slice_fusion.3
  1248.9 2.2 fusion.16
  1253.2 139.4 %all-reduce.19.cloned.1.call-done = f32[512,128]{1,0:T(8,128)} async-done(((f32[512,128]{1,0:T(8,128)}), f32[512,128]{1,0:T(8,128)}) %all-reduce.19.cloned.1.call-update) | async-done | bytes 262160 | tf_op jit(solution)/shard_map/psum | solution.py:121
  1392.6 3.4 bitcast_dynamic-update-slice_fusion.2
  1396.1 2.2 fusion.14
  1399.0 2.2 constant_dynamic-slice_fusion.1
  1402.6 13.7 reshape.130
  1416.4 123.4 %all-reduce.21.cloned.1.call-done = f32[512,128]{1,0:T(8,128)} async-done(((f32[512,128]{1,0:T(8,128)}), f32[512,128]{1,0:T(8,128)}) %all-reduce.21.cloned.1.call-update) | async-done | bytes 262160 | tf_op jit(solution)/shard_map/psum | solution.py:121
  1539.8 3.4 fusion.12
  1543.1 3.0 copy.42
  (118 shorter events, 52.0 us)
Async XLA Ops:
  7.2 7.6 copy-start.8
  156.6 101.7 %all-to-all-start.1 = ((f32[1,2048,1024]{2,0,1:T(1,128)}), f32[1,2048,1024]{2,0,1:T(1,128)}, u32[]{:S(2)}, u32[]{:S(2)}) async-start(f32[1,2048,1024]{2,0,1:T(1,128)} %copy.31), calls=%async_computation.1 | async-start | bytes 16777216 | tf_op jit(solution)/shard_map/all_to_all | solution.py:60
  163.8 254.8 %all-reduce.9.cloned.1.call-start = ((), (), s32[]{:S(2)}) async-start(), calls=%async_computation.2 | async-start | bytes 2097152 | tf_op jit(solution)/shard_map/psum | solution.py:71
  272.2 290.4 %all-reduce.11.cloned.1.call-start = ((), (), s32[]{:S(2)}) async-start(), calls=%async_computation.3 | async-start | bytes 8388608 | tf_op jit(solution)/shard_map/psum | solution.py:73
  273.0 455.7 %all-reduce.13.cloned.1.call-start = ((), (), s32[]{:S(2)}) async-start(), calls=%async_computation.5 | async-start | bytes 524288 | tf_op jit(solution)/shard_map/psum | solution.py:121
  560.4 1.5 copy-start.4
  561.9 0.6 copy-start.6
  562.6 5.7 copy-start.3
  570.6 7.5 copy-start.1
  573.7 4.4 copy-start.2
  586.8 323.1 %all-gather.2.cloned.1.call-start = ((), (), s32[]{:S(2)}) async-start(), calls=%async_computation.4 | async-start | bytes 18874368 | tf_op jit(solution)/shard_map/all_gather | solution.py:9
  593.0 6.8 copy-start.5
  593.0 6.9 copy-start.7
  599.1 499.3 %all-reduce.15.cloned.1.call-start = ((), (), s32[]{:S(2)}) async-start(), calls=%async_computation.6 | async-start | bytes 524288 | tf_op jit(solution)/shard_map/psum | solution.py:121
  951.7 3.2 copy-start
  956.7 288.8 %all-reduce.17.cloned.1.call-start = ((), (), s32[]{:S(2)}) async-start(), calls=%async_computation.7 | async-start | bytes 524288 | tf_op jit(solution)/shard_map/psum | solution.py:121
  1104.8 287.8 %all-reduce.19.cloned.1.call-start = ((), (), s32[]{:S(2)}) async-start(), calls=%async_computation.8 | async-start | bytes 524288 | tf_op jit(solution)/shard_map/psum | solution.py:121
  1251.9 287.9 %all-reduce.21.cloned.1.call-start = ((), (), s32[]{:S(2)}) async-start(), calls=%async_computation.9 | async-start | bytes 524288 | tf_op jit(solution)/shard_map/psum | solution.py:121
Sparse Core Ops, SparseCore 0:
  272.3 146.2 all-reduce.8
  421.7 128.4 all-reduce.10
  586.9 141.6 all-reduce.12
  730.8 179.0 all-gather.1
  956.8 141.5 all-reduce.14
  1105.0 140.4 all-reduce.16
  1252.0 140.5 all-reduce.18
  1399.2 140.5 all-reduce.20
